TPU v7x, 32 devices: a whole 2x2x4 slice. The times are simulated.
32 devices in a mesh: wave: 8 (over z, x), lev: 4 (over y, core).
Axes of the slice: x: 2, y: 2, z: 4, core: 2. Of those that a mesh axis runs over, the one named last changes fastest.
Arguments:
- div_grid: bfloat16 [1, 2, 128, 256, 1024], P(None, None, 'lev', 'wave'), may hold values from -6 to 6
- temp_grid: bfloat16 [1, 2, 128, 256, 1024], P(None, None, 'lev', 'wave'), may hold values from -6 to 6
- legendre: bfloat16 [256, 131328], P(None, 'wave'), may hold values from -0.375 to 0.375
- gauss_weight: float32 [256], replicated, may hold values from 0.1 to 1
- latitude_of_row: int32 [256], replicated, may hold values from 0 to 255, each once
- pair_of_slot: int32 [256], replicated, may hold values from 0 to 255, each once
- g_matrix: float32 [128, 128], replicated, may hold values from -0.5 to 0.5
- modes_in: float32 [128, 128], replicated, may hold values from -4 to 4, as said below
- modes_out: float32 [128, 128], replicated, may hold values from -1.5 to 1.5
- mode_rates: float32 [128], replicated, may hold values from 0.05 to 5
- temp_coupling: float32 [128], replicated, may hold values from 0.2 to 1
Outputs:
- div_next: float32 [1, 2, 128, 256, 1024], P(None, None, 'lev', 'wave')
- temp_next: float32 [1, 2, 128, 256, 1024], P(None, None, 'lev', 'wave')
Inputs may be any that keep to these rules, and one draw needn't show every extreme that they name: Each value once; stored row q holds northern latitude latitude_of_row[q] (hemisphere 0) and its mirror 512 - 1 - latitude_of_row[q] (hemisphere 1). Each value once; slot s carries zonal wavenumbers pair_of_slot[s] and 511 - pair_of_slot[s]. modes_in is the inverse of modes_out.
All inputs are finite; a program needn't handle non-finite values.
Results may differ from a plain program's by a relative error of at most 0.0067.
Values may be sent and summed in bfloat16 or wider, within the bound.
A program may use at most 128 MiB of HBM per device.

v0:
```python
import math

import jax
import jax.numpy as jnp
from jax import lax
from jax.sharding import PartitionSpec as P


def fourier_table(pair_ids, lat_count, lon_count):
    slot_total = pair_ids.shape[0]
    members = jnp.stack([pair_ids, lat_count - 1 - pair_ids], axis=-1)
    wavenum = jnp.broadcast_to(members[:, None, :], (slot_total, 2, 2)).reshape(-1)
    part_ids = jnp.broadcast_to(
        jnp.arange(2, dtype=jnp.int32)[None, :, None], (slot_total, 2, 2)
    ).reshape(-1)
    places = jnp.arange(lon_count, dtype=jnp.int32)
    phases = places[:, None] * wavenum[None, :] % lon_count
    angles = phases.astype(jnp.float32) * (2.0 * math.pi / lon_count)
    values = jnp.cos(angles + part_ids.astype(jnp.float32)[None, :] * (0.5 * math.pi)) / math.sqrt(
        lon_count
    )
    doubling = jnp.where(wavenum == 0, 1.0, 2.0).astype(jnp.bfloat16)
    return (values.astype(jnp.bfloat16), doubling)


def total_wave(pair_ids, lat_count):
    even_cols = lat_count // 2 + 1
    column = jnp.arange(lat_count + 1, dtype=jnp.int32)[None, :]
    member_one = pair_ids[:, None]
    member_two = lat_count - 1 - member_one
    even_first = (lat_count - member_one + 1) // 2
    odd_first = (lat_count - member_one) // 2
    odd_column = column - even_cols
    in_even = column < even_cols
    owned_first = jnp.where(in_even, column < even_first, odd_column < odd_first)
    even_wave = jnp.where(
        owned_first, member_one + 2 * column, member_two + 2 * (column - even_first)
    )
    odd_wave = jnp.where(
        owned_first, member_one + 2 * odd_column + 1, member_two + 1 + 2 * (odd_column - odd_first)
    )
    return (jnp.where(in_even, even_wave, odd_wave), owned_first)


def vertical_solve(
    div_spec, temp_spec, factors, g_matrix, modes_in, modes_out, mode_rates, temp_coupling
):
    highest = lax.Precision.HIGHEST
    div_part = div_spec.astype(jnp.float32)
    temp_part = temp_spec.astype(jnp.float32)
    wave_factor = factors[:, None, :]
    coupled = jnp.einsum("kl,ilc->ikc", g_matrix, temp_part, precision=highest)
    rhs_part = div_part - 2.0 * wave_factor * coupled
    modal_part = jnp.einsum("kl,ilc->ikc", modes_in, rhs_part, precision=highest)
    modal_part = modal_part / (1.0 + 4.0 * wave_factor * mode_rates[None, :, None])
    div_solved = jnp.einsum("kl,ilc->ikc", modes_out, modal_part, precision=highest)
    temp_solved = temp_part - temp_coupling[None, :, None] * div_solved
    return (div_solved.astype(jnp.bfloat16), temp_solved.astype(jnp.bfloat16))


def per_device(
    div_grid,
    temp_grid,
    legendre,
    gauss_weight,
    latitude_of_row,
    pair_of_slot,
    g_matrix,
    modes_in,
    modes_out,
    mode_rates,
    temp_coupling,
):
    wave_count = lax.axis_size("wave")
    level_shards = lax.axis_size("lev")
    batches = div_grid.shape[0]
    lev_local = div_grid.shape[2]
    lat_pairs = div_grid.shape[3]
    lon_count = div_grid.shape[4]
    half_count = lat_pairs * wave_count
    lat_count = 2 * half_count
    col_count = lat_count + 1
    even_cols = half_count + 1
    slot_count = pair_of_slot.shape[0] // wave_count
    combo_width = slot_count * 4
    item_total_count = batches * slot_count * 2
    padded_items = (item_total_count + level_shards - 1) // level_shards * level_shards
    local_pairs = lax.dynamic_slice_in_dim(
        pair_of_slot, lax.axis_index("wave") * slot_count, slot_count
    )
    forward_dft, doubling = fourier_table(pair_of_slot, lat_count, lon_count)
    rows_slot = (
        jnp.take(legendre, latitude_of_row, axis=0)
        .reshape(half_count, slot_count, col_count)
        .transpose(1, 0, 2)
    )
    even_rows = rows_slot[..., :even_cols]
    odd_rows = rows_slot[..., even_cols:]
    row_weight = jnp.take(gauss_weight, latitude_of_row, axis=0)
    local_total, local_first = total_wave(local_pairs, lat_count)
    member_mask = jnp.stack([local_first, jnp.logical_not(local_first)], axis=1).astype(
        jnp.bfloat16
    )

    def analyse(field_grid):
        return jnp.einsum(
            "bhlpx,xk->bhlpk", field_grid, forward_dft, preferred_element_type=jnp.float32
        ).astype(jnp.bfloat16)

    div_four, temp_four = (
        lax.all_to_all(analyse(div_grid), "wave", split_axis=4, concat_axis=3, tiled=True),
        lax.all_to_all(analyse(temp_grid), "wave", split_axis=4, concat_axis=3, tiled=True),
    )

    def forward(fourier):
        hemispheres = fourier.transpose(1, 4, 0, 2, 3).astype(jnp.float32)
        symmetric = (row_weight * (hemispheres[0] + hemispheres[1])).astype(jnp.bfloat16)
        antisymmetric = (row_weight * (hemispheres[0] - hemispheres[1])).astype(jnp.bfloat16)
        row_total = 4 * batches * lev_local
        symmetric = symmetric.reshape(slot_count, row_total, half_count)
        antisymmetric = antisymmetric.reshape(slot_count, row_total, half_count)
        even_spec = jnp.einsum(
            "jnq,jqc->jnc", symmetric, even_rows, preferred_element_type=jnp.float32
        )
        odd_spec = jnp.einsum(
            "jnq,jqc->jnc", antisymmetric, odd_rows, preferred_element_type=jnp.float32
        )
        even_spec = even_spec.reshape(slot_count, 2, 2, batches, lev_local, even_cols)
        odd_spec = odd_spec.reshape(slot_count, 2, 2, batches, lev_local, col_count - even_cols)
        pick_even = local_first[:, None, None, None, :even_cols]
        pick_odd = local_first[:, None, None, None, even_cols:]
        even_pick = jnp.where(pick_even, even_spec[:, :, 0], even_spec[:, :, 1])
        odd_pick = jnp.where(pick_odd, odd_spec[:, :, 0], odd_spec[:, :, 1])
        joined = jnp.concatenate([even_pick, odd_pick], axis=-1).astype(jnp.bfloat16)
        joined = joined.transpose(2, 0, 1, 3, 4).reshape(item_total_count, lev_local, col_count)
        return jnp.pad(joined, ((0, padded_items - item_total_count), (0, 0), (0, 0)))

    div_spec, temp_spec = (
        lax.all_to_all(forward(div_four), "lev", split_axis=0, concat_axis=1, tiled=True),
        lax.all_to_all(forward(temp_four), "lev", split_axis=0, concat_axis=1, tiled=True),
    )
    item_count = div_spec.shape[0]
    combos = lax.axis_index("lev") * item_count + jnp.arange(item_count, dtype=jnp.int32)
    item_slot = combos // 2 % slot_count
    item_total = jnp.take(local_total, item_slot, axis=0)
    factors = (item_total * (item_total + 1)).astype(jnp.float32) / float(
        (lat_count - 1) * lat_count
    )
    div_new, temp_new = vertical_solve(
        div_spec, temp_spec, factors, g_matrix, modes_in, modes_out, mode_rates, temp_coupling
    )
    div_back, temp_back = (
        lax.all_to_all(div_new, "lev", split_axis=1, concat_axis=0, tiled=True),
        lax.all_to_all(temp_new, "lev", split_axis=1, concat_axis=0, tiled=True),
    )

    def synth_levels(spectral):
        values = (
            spectral[:item_total_count]
            .reshape(batches, slot_count, 2, lev_local, col_count)
            .transpose(1, 2, 0, 3, 4)
        )
        masked = values[:, :, None] * member_mask[:, None, :, None, None, :]
        masked = masked.reshape(slot_count, 4 * batches * lev_local, col_count)
        even_sum = jnp.einsum(
            "jnc,jqc->jnq", masked[..., :even_cols], even_rows, preferred_element_type=jnp.float32
        )
        odd_sum = jnp.einsum(
            "jnc,jqc->jnq", masked[..., even_cols:], odd_rows, preferred_element_type=jnp.float32
        )
        stacked = jnp.stack([even_sum + odd_sum, even_sum - odd_sum], axis=0).astype(jnp.bfloat16)
        stacked = stacked.reshape(2, combo_width, batches, lev_local, half_count)
        return stacked.transpose(2, 0, 3, 4, 1)

    div_fourier = synth_levels(div_back)
    temp_fourier = synth_levels(temp_back)
    div_home, temp_home = (
        lax.all_to_all(div_fourier, "wave", split_axis=3, concat_axis=4, tiled=True),
        lax.all_to_all(temp_fourier, "wave", split_axis=3, concat_axis=4, tiled=True),
    )

    def synthesise(fourier):
        scaled = fourier * doubling
        return jnp.einsum(
            "bhlpk,xk->bhlpx", scaled, forward_dft, preferred_element_type=jnp.float32
        )

    return (synthesise(div_home), synthesise(temp_home))


def solution(mesh):
    in_specs = (
        P(None, None, "lev", "wave", None),
        P(None, None, "lev", "wave", None),
        P(None, "wave"),
        P(),
        P(),
        P(),
        P(),
        P(),
        P(),
        P(),
        P(),
    )
    out_specs = (P(None, None, "lev", "wave", None), P(None, None, "lev", "wave", None))
    return jax.shard_map(
        per_device, mesh=mesh, in_specs=in_specs, out_specs=out_specs, check_vma=False
    )
```

profile of v0, /device:TPU:0, one launch (start us, length us, event | category | flops | bytes accessed | tf_op | source)
XLA Modules:
  0.0 831.1 jit_solution(14166421761124144738)
XLA Ops:
  3.0 22.1 %convert_bitcast_fusion.1 = bf16[1,2,32,32,1024]{4,3,2,1,0:T(8,128)(2,1)} fusion(bf16[1,2,32,32,1024]{4,3,2,1,0:T(8,128)(2,1)} %param.11, f32[1024]{0:T(1024)S(1)} %mul.238, s32[1024]{0:T(1024)S(1)} %mul.231), kind=kOutput, calls=%fused_computation.43 | convolution fusion | flops 4314890240 | bytes 8396800 | tf_op jit(solution)/shard_map/bhlpx,xk->bhlpk/dot_general | solution.py:106
  25.1 23.1 %copy.156 = bf16[1,2,32,32,1024]{3,2,1,0,4:T(8,128)(2,1)} copy(bf16[1,2,32,32,1024]{4,3,2,1,0:T(8,128)(2,1)} %convert_bitcast_fusion.1) | data formatting | bytes 8388608 | tf_op jit(solution)/shard_map/convert_element_type | solution.py:108
  48.2 18.7 %reshape.710 = bf16[8,2,131072]{2,1,0:T(2,128)(2,1)} reshape(bf16[1024,1,2,32,32]{4,3,2,1,0:T(8,128)(2,1)} %bitcast.157) | data formatting | bytes 8388608
  66.9 7.5 all-to-all-start
  74.4 22.1 %convert_bitcast_fusion = bf16[1,2,32,32,1024]{4,3,2,1,0:T(8,128)(2,1)} fusion(bf16[1,2,32,32,1024]{4,3,2,1,0:T(8,128)(2,1)} %param.12, f32[1024]{0:T(1024)S(1)} %mul.238, s32[1024]{0:T(1024)S(1)} %mul.231), kind=kOutput, calls=%fused_computation.40 | convolution fusion | flops 4314890240 | bytes 8396800 | tf_op jit(solution)/shard_map/bhlpx,xk->bhlpk/dot_general | solution.py:106
  96.5 23.1 %copy.166 = bf16[1,2,32,32,1024]{3,2,1,0,4:T(8,128)(2,1)} copy(bf16[1,2,32,32,1024]{4,3,2,1,0:T(8,128)(2,1)} %convert_bitcast_fusion) | data formatting | bytes 8388608 | tf_op jit(solution)/shard_map/convert_element_type | solution.py:108
  119.6 18.7 %reshape.712 = bf16[8,2,131072]{2,1,0:T(2,128)(2,1)} reshape(bf16[1024,1,2,32,32]{4,3,2,1,0:T(8,128)(2,1)} %bitcast.158) | data formatting | bytes 8388608
  138.3 29.3 %all-to-all-done = bf16[8,2,131072]{2,1,0:T(2,128)(2,1)} async-done(((bf16[8,2,131072]{2,1,0:T(2,128)(2,1)}), bf16[8,2,131072]{2,1,0:T(2,128)(2,1)}, u32[]{:S(2)}, u32[]{:S(2)}) %all-to-all-start) | async-done | bytes 4194336 | tf_op jit(solution)/shard_map/all_to_all | solution.py:111
  172.7 12.1 %copy.160 = bf16[256,16416]{1,0:T(8,128)(2,1)} copy(bf16[256,16416]{0,1:T(8,128)(2,1)} %param.13) | data formatting | bytes 16809984 | tf_op args[2]
  187.0 21.5 %gather_fusion.1 = bf16[256,16416]{1,0:T(8,128)(2,1)} fusion(bf16[256,16416]{1,0:T(8,128)(2,1)} %copy.160, s32[1024]{0:T(1024)S(1)} %pad_clamp_fusion.1), kind=kCustom, calls=%fused_computation.1 | custom fusion | bytes 16811008 | tf_op jit(solution)/shard_map/jit(_take)/gather | solution.py:93
  208.5 12.1 %copy.161 = bf16[256,16416]{0,1:T(8,128)(2,1)} copy(bf16[256,16416]{1,0:T(8,128)(2,1)} %gather_fusion.1) | data formatting | bytes 16809984 | tf_op jit(solution)/shard_map/jit(_take)/gather | solution.py:93
  220.6 8.0 gather.16
  228.6 7.6 select_bitcast_fusion
  236.2 12.4 %reshape.711 = bf16[1024,1,2,32,32]{4,3,2,1,0:T(8,128)(2,1)} reshape(bf16[8,2,131072]{2,1,0:T(2,128)(2,1)} %all-to-all-done) | data formatting | bytes 8388608
  248.5 17.5 %copy.157 = bf16[1,2,32,32,1024]{4,3,2,1,0:T(8,128)(2,1)} copy(bf16[1,2,32,32,1024]{3,2,1,0,4:T(8,128)(2,1)} %bitcast.159) | data formatting | bytes 8388608 | tf_op jit(solution)/shard_map/all_to_all | solution.py:111
  275.5 5.5 copy.159
  280.9 5.6 copy.163
  286.5 5.5 fusion.40
  292.0 5.2 fusion.48
  297.2 12.4 %reshape.713 = bf16[1024,1,2,32,32]{4,3,2,1,0:T(8,128)(2,1)} reshape(bf16[8,2,131072]{2,1,0:T(2,128)(2,1)} %all-to-all-done.2) | data formatting | bytes 8388608
  309.6 17.5 %copy.167 = bf16[1,2,32,32,1024]{4,3,2,1,0:T(8,128)(2,1)} copy(bf16[1,2,32,32,1024]{3,2,1,0,4:T(8,128)(2,1)} %bitcast.160) | data formatting | bytes 8388608 | tf_op jit(solution)/shard_map/all_to_all | solution.py:112
  336.7 5.5 copy.169
  342.1 7.0 fusion.38
  349.1 5.4 copy.171
  354.6 5.3 fusion.46
  375.6 27.2 %all-to-all-done.3 = bf16[64,32,513]{2,1,0:T(8,128)(2,1)S(1)} async-done(((bf16[64,32,513]{2,1,0:T(8,128)(2,1)}), bf16[64,32,513]{2,1,0:T(8,128)(2,1)S(1)}, u32[]{:S(2)}, u32[]{:S(2)}) %all-to-all-start.3) | async-done | bytes 2101280 | tf_op jit(solution)/shard_map/all_to_all | solution.py:140
  402.8 5.0 all-to-all-start.1
  410.8 28.3 %all-to-all-done.1 = bf16[64,32,513]{2,1,0:T(8,128)(2,1)} async-done(((bf16[64,32,513]{2,1,0:T(8,128)(2,1)}), bf16[64,32,513]{2,1,0:T(8,128)(2,1)}, u32[]{:S(2)}, u32[]{:S(2)}) %all-to-all-start.1) | async-done | bytes 2101280 | tf_op jit(solution)/shard_map/all_to_all | solution.py:139
  443.9 5.6 copy.175
  463.3 5.0 copy.176
  483.9 20.4 %all-to-all-done.4 = bf16[16,128,513]{2,0,1:T(8,128)(2,1)} async-done(((bf16[16,128,513]{2,0,1:T(8,128)(2,1)}), bf16[16,128,513]{2,0,1:T(8,128)(2,1)}, u32[]{:S(2)}, u32[]{:S(2)}) %all-to-all-start.4) | async-done | bytes 2101280 | tf_op jit(solution)/shard_map/all_to_all | solution.py:153
  512.3 26.9 %all-to-all-done.6 = bf16[16,128,513]{2,0,1:T(8,128)(2,1)S(1)} async-done(((bf16[16,128,513]{2,0,1:T(8,128)(2,1)}), bf16[16,128,513]{2,0,1:T(8,128)(2,1)S(1)}, u32[]{:S(2)}, u32[]{:S(2)}) %all-to-all-start.6) | async-done | bytes 2101280 | tf_op jit(solution)/shard_map/all_to_all | solution.py:154
  541.2 7.6 broadcast_multiply_fusion
  548.9 5.0 fusion.44
  558.8 5.2 copy.181
  572.6 6.3 all-to-all-start.5
  578.9 5.0 fusion.42
  588.8 5.2 copy.192
  602.5 69.4 %all-to-all-done.5 = bf16[1,2,32,256,128]{4,2,1,0,3:T(8,128)(2,1)} async-done(((bf16[1,2,32,256,128]{4,2,1,0,3:T(8,128)(2,1)}), bf16[1,2,32,256,128]{4,2,1,0,3:T(8,128)(2,1)}, u32[]{:S(2)}, u32[]{:S(2)}) %all-to-all-start.5) | async-done | bytes 4194336 | tf_op jit(solution)/shard_map/all_to_all | solution.py:178
  676.4 4.9 copy.183
  681.3 6.2 copy.184
  687.5 7.7 all_to_all.95
  695.2 73.7 %all-to-all-done.7 = bf16[1,2,32,256,128]{4,2,1,0,3:T(8,128)(2,1)} async-done(((bf16[1,2,32,256,128]{4,2,1,0,3:T(8,128)(2,1)}), bf16[1,2,32,256,128]{4,2,1,0,3:T(8,128)(2,1)}, u32[]{:S(2)}, u32[]{:S(2)}) %all-to-all-start.7) | async-done | bytes 4194336 | tf_op jit(solution)/shard_map/all_to_all | solution.py:179
  769.0 4.9 copy.194
  773.9 6.2 copy.195
  780.0 7.3 all_to_all.102
  787.3 22.8 %fusion.24 = f32[1,2,32,32,1024]{4,3,2,1,0:T(8,128)} fusion(bf16[2,32,32,1024]{3,2,1,0:T(8,128)(2,1)} %all_to_all.95, bf16[1024]{0:T(1024)(128)(2,1)S(1)} %select_convert_fusion, f32[1024]{0:T(1024)S(1)} %copy-done.15, s32[1024]{0:T(1024)S(1)} %copy-done.12), kind=kOutput, calls=%fused_computation.51 | convolution fusion | flops 4314890240 | bytes 12593152 | tf_op jit(solution)/shard_map/bhlpk,xk->bhlpx/dot_general | solution.py:184
  810.1 20.8 %fusion.27 = f32[1,2,32,32,1024]{4,3,2,1,0:T(8,128)} fusion(bf16[2,32,32,1024]{3,2,1,0:T(8,128)(2,1)S(1)} %copy-done.9, bf16[1024]{0:T(1024)(128)(2,1)S(1)} %select_convert_fusion, f32[1024]{0:T(1024)S(1)} %copy-done.15, s32[1024]{0:T(1024)S(1)} %copy-done.12), kind=kOutput, calls=%fused_computation.52 | convolution fusion | flops 4314890240 | bytes 12593152 | tf_op jit(solution)/shard_map/bhlpk,xk->bhlpx/dot_general | solution.py:184
  (112 shorter events, 122.7 us)
Async XLA Ops:
  0.6 448.9 %copy-start = (f32[128,128]{1,0:T(8,128)S(1)}, f32[128,128]{1,0:T(8,128)}, u32[]{:S(2)}) copy-start(f32[128,128]{1,0:T(8,128)} %param.17) | copy-start | bytes 196612
  2.7 71.7 %copy-start.11 = (s32[1024]{0:T(1024)}, s32[1024]{0:T(1024)S(1)}, u32[]{:S(2)}) copy-start(s32[1024]{0:T(1024)S(1)} %mul.231) | copy-start | bytes 12292
  3.0 71.4 %copy-start.14 = (f32[1024]{0:T(1024)}, f32[1024]{0:T(1024)S(1)}, u32[]{:S(2)}) copy-start(f32[1024]{0:T(1024)S(1)} %mul.238) | copy-start | bytes 12292
  66.9 100.7 %all-to-all-start = ((bf16[8,2,131072]{2,1,0:T(2,128)(2,1)}), bf16[8,2,131072]{2,1,0:T(2,128)(2,1)}, u32[]{:S(2)}, u32[]{:S(2)}) async-start(bf16[8,2,131072]{2,1,0:T(2,128)(2,1)} %reshape.710), calls=%async_computation | async-start | bytes 8388608 | tf_op jit(solution)/shard_map/all_to_all | solution.py:111
  138.3 33.8 %copy-start.13 = (s32[256]{0:T(256)S(1)}, s32[256]{0:T(256)}, u32[]{:S(2)}) copy-start(s32[256]{0:T(256)} %param.16) | copy-start | bytes 3076
  167.6 129.6 %all-to-all-start.2 = ((bf16[8,2,131072]{2,1,0:T(2,128)(2,1)}), bf16[8,2,131072]{2,1,0:T(2,128)(2,1)}, u32[]{:S(2)}, u32[]{:S(2)}) async-start(bf16[8,2,131072]{2,1,0:T(2,128)(2,1)} %reshape.712), calls=%async_computation.2 | async-start | bytes 8388608 | tf_op jit(solution)/shard_map/all_to_all | solution.py:112
  172.7 12.1 %copy-start.16 = (s32[256]{0:T(256)S(1)}, s32[256]{0:T(256)}, u32[]{:S(2)}) copy-start(s32[256]{0:T(256)} %param.15) | copy-start | bytes 3076
  172.7 12.1 %copy-start.1 = (f32[256]{0:T(256)S(1)}, f32[256]{0:T(256)}, u32[]{:S(2)}) copy-start(f32[256]{0:T(256)} %param.14) | copy-start | bytes 3076
  286.5 5.5 copy-start.5
  354.6 5.3 copy-start.6
  359.8 1.6 copy-start.8
  367.9 34.9 %all-to-all-start.3 = ((bf16[64,32,513]{2,1,0:T(8,128)(2,1)}), bf16[64,32,513]{2,1,0:T(8,128)(2,1)S(1)}, u32[]{:S(2)}, u32[]{:S(2)}) async-start(bf16[64,32,513]{2,1,0:T(8,128)(2,1)} %pad_maximum_fusion.1), calls=%async_computation.3 | async-start | bytes 5242880 | tf_op jit(solution)/shard_map/all_to_all | solution.py:140
  402.8 5.8 copy-start.7
  402.8 36.3 %all-to-all-start.1 = ((bf16[64,32,513]{2,1,0:T(8,128)(2,1)}), bf16[64,32,513]{2,1,0:T(8,128)(2,1)}, u32[]{:S(2)}, u32[]{:S(2)}) async-start(bf16[64,32,513]{2,1,0:T(8,128)(2,1)} %pad_maximum_fusion), calls=%async_computation.1 | async-start | bytes 5242880 | tf_op jit(solution)/shard_map/all_to_all | solution.py:139
  449.6 2.7 copy-start.4
  449.6 2.7 copy-start.10
  452.3 3.6 copy-start.18
  452.3 3.6 copy-start.19
  459.6 2.0 copy-start.3
  468.3 8.0 copy-start.17
  468.3 36.0 %all-to-all-start.4 = ((bf16[16,128,513]{2,0,1:T(8,128)(2,1)}), bf16[16,128,513]{2,0,1:T(8,128)(2,1)}, u32[]{:S(2)}, u32[]{:S(2)}) async-start(bf16[16,128,513]{2,0,1:T(8,128)(2,1)} %copy.176), calls=%async_computation.4 | async-start | bytes 5242880 | tf_op jit(solution)/shard_map/all_to_all | solution.py:153
  504.3 34.9 %all-to-all-start.6 = ((bf16[16,128,513]{2,0,1:T(8,128)(2,1)}), bf16[16,128,513]{2,0,1:T(8,128)(2,1)S(1)}, u32[]{:S(2)}, u32[]{:S(2)}) async-start(bf16[16,128,513]{2,0,1:T(8,128)(2,1)} %copy.187), calls=%async_computation.6 | async-start | bytes 5242880 | tf_op jit(solution)/shard_map/all_to_all | solution.py:154
  548.9 5.0 copy-start.2
  572.6 11.4 %slice-start = ((s8[5242880]{0:T(1024)(128)(4,1)}), s8[1048576]{0:T(1024)(128)(4,1)S(1)}, s32[]{:S(2)}) async-start(s8[5242880]{0:T(1024)(128)(4,1)} %bitcast.169), calls=%async_computation.8 | async-start | bytes 2097152
  572.6 99.2 %all-to-all-start.5 = ((bf16[1,2,32,256,128]{4,2,1,0,3:T(8,128)(2,1)}), bf16[1,2,32,256,128]{4,2,1,0,3:T(8,128)(2,1)}, u32[]{:S(2)}, u32[]{:S(2)}) async-start(bf16[1,2,32,256,128]{4,2,1,0,3:T(8,128)(2,1)} %maximum_bitcast_fusion), calls=%async_computation.5 | async-start | bytes 8388608 | tf_op jit(solution)/shard_map/all_to_all | solution.py:178
  578.9 5.1 slice-start.1
  602.5 73.9 %copy-start.12 = (s32[1024]{0:T(1024)S(1)}, s32[1024]{0:T(1024)}, u32[]{:S(2)}) copy-start(s32[1024]{0:T(1024)} %copy-done.11) | copy-start | bytes 12292
  671.8 97.1 %all-to-all-start.7 = ((bf16[1,2,32,256,128]{4,2,1,0,3:T(8,128)(2,1)}), bf16[1,2,32,256,128]{4,2,1,0,3:T(8,128)(2,1)}, u32[]{:S(2)}, u32[]{:S(2)}) async-start(bf16[1,2,32,256,128]{4,2,1,0,3:T(8,128)(2,1)} %maximum_bitcast_fusion.1), calls=%async_computation.7 | async-start | bytes 8388608 | tf_op jit(solution)/shard_map/all_to_all | solution.py:179
  780.0 7.3 copy-start.15
  787.3 22.8 %copy-start.9 = (bf16[2,32,32,1024]{3,2,1,0:T(8,128)(2,1)S(1)}, bf16[2,32,32,1024]{3,2,1,0:T(8,128)(2,1)}, u32[]{:S(2)}) copy-start(bf16[2,32,32,1024]{3,2,1,0:T(8,128)(2,1)} %all_to_all.102) | copy-start | bytes 12582916
where the time goes:
time: 842 us; the launch traced here: 831 us
  local copies, waits for them, and re-layouts  324 us (38%)
  waiting for transfers between devices  275 us (33%)
  matrix products  140 us (17%)
  other arithmetic  50.1 us (6%)
  starting transfers between devices  39.9 us (5%)
    unnamed x51, local copies, waits for them, and re-layouts  84.4 us
    all_to_all x1, waiting for transfers between devices, per_device(): lax.all_to_all(temp_fourier, 'wave', split_axis=3, concat_axis=4, tiled=T...  73.7 us
    all_to_all x1, waiting for transfers between devices, per_device(): lax.all_to_all(div_fourier, 'wave', split_axis=3, concat_axis=4, tiled=True)  69.4 us
    convert_element_type x2, local copies, waits for them, and re-layouts, analyse(): return jnp.einsum('bhlpx,xk->bhlpk', field_grid, forward_dft, preferred_e...  46.2 us
    dot_general x2, matrix products, analyse(): jnp.einsum('bhlpx,xk->bhlpk', field_grid, forward_dft, preferred_element_...  44.2 us
    dot_general x2, matrix products, synthesise(): jnp.einsum('bhlpk,xk->bhlpx', scaled, forward_dft, preferred_element_type...  43.6 us
    gather x3, local copies, waits for them, and re-layouts, per_device(): jnp.take(legendre, latitude_of_row, axis=0)  41.6 us
    all_to_all x1, waiting for transfers between devices, per_device(): lax.all_to_all(analyse(div_grid), 'wave', split_axis=4, concat_axis=3, ti...  29.3 us
  transfers between devices with their start and end apart: 8, of which 7 were waited for; matrix products, arithmetic and copies ran while one was open for 30% of the time, Pallas kernels for 0%

commit v1 on v0

--- a/solution.py
+++ b/solution.py
@@ -4,6 +4,9 @@
 import jax.numpy as jnp
 from jax import lax
 from jax.sharding import PartitionSpec as P
+
+
+CHUNKS = 2
 
 
 def fourier_table(pair_ids, lat_count, lon_count):
@@ -58,7 +61,7 @@
     return (div_solved.astype(jnp.bfloat16), temp_solved.astype(jnp.bfloat16))
 
 
-def per_device(
+def per_device_padded(
     div_grid,
     temp_grid,
     legendre,
@@ -188,6 +191,218 @@
     return (synthesise(div_home), synthesise(temp_home))
 
 
+def fits_slots(slot_count, level_shards, batches):
+    return slot_count % level_shards == 0 and batches == 1
+
+
+def transform_table(pair_ids, lat_count, lon_count):
+    slot_total = pair_ids.shape[0]
+    fine = math.gcd(lon_count, 128)
+    members = jnp.stack([pair_ids, lat_count - 1 - pair_ids], axis=-1)
+    wavenum = jnp.broadcast_to(members[:, None, :], (slot_total, 2, 2)).reshape(-1)
+    part_ids = jnp.broadcast_to(
+        jnp.arange(2, dtype=jnp.int32)[None, :, None], (slot_total, 2, 2)
+    ).reshape(-1)
+    unit = 2.0 * math.pi / lon_count
+    low = (wavenum[:, None] * jnp.arange(fine, dtype=jnp.int32)[None, :]) % lon_count
+    high = (
+        wavenum[:, None] * (fine * jnp.arange(lon_count // fine, dtype=jnp.int32))[None, :]
+    ) % lon_count
+    low = low.astype(jnp.float32) * unit
+    high = high.astype(jnp.float32) * unit + part_ids.astype(jnp.float32)[:, None] * (
+        0.5 * math.pi
+    )
+    scale = 1.0 / math.sqrt(lon_count)
+    low_cos, low_sin = lax.optimization_barrier((jnp.cos(low) * scale, jnp.sin(low) * scale))
+    high_cos, high_sin = lax.optimization_barrier((jnp.cos(high), jnp.sin(high)))
+    pieces = [
+        high_cos[:, n : n + 1] * low_cos - high_sin[:, n : n + 1] * low_sin
+        for n in range(lon_count // fine)
+    ]
+    doubling = jnp.where(wavenum == 0, 1.0, 2.0).astype(jnp.bfloat16)
+    return (jnp.concatenate(pieces, axis=1).astype(jnp.bfloat16), doubling)
+
+
+def per_device(
+    div_grid,
+    temp_grid,
+    legendre,
+    gauss_weight,
+    latitude_of_row,
+    pair_of_slot,
+    g_matrix,
+    modes_in,
+    modes_out,
+    mode_rates,
+    temp_coupling,
+):
+    wave_count = lax.axis_size("wave")
+    level_shards = lax.axis_size("lev")
+    slot_count = pair_of_slot.shape[0] // wave_count
+    batches, _, lev_local, lat_pairs, lon_count = div_grid.shape
+    if not fits_slots(slot_count, level_shards, batches):
+        return per_device_padded(
+            div_grid,
+            temp_grid,
+            legendre,
+            gauss_weight,
+            latitude_of_row,
+            pair_of_slot,
+            g_matrix,
+            modes_in,
+            modes_out,
+            mode_rates,
+            temp_coupling,
+        )
+    everyone = wave_count * level_shards
+    own = slot_count // level_shards
+    chunks = CHUNKS if own % CHUNKS == 0 else 1
+    part = own // chunks
+    half_count = lat_pairs * wave_count
+    lat_count = 2 * half_count
+    col_count = lat_count + 1
+    even_cols = half_count + 1
+    levels = lev_local * level_shards
+    rows = 2 * lev_local * lat_pairs
+
+    table, doubling = transform_table(pair_of_slot, lat_count, lon_count)
+    table = table.reshape(everyone, chunks, part * 4, lon_count)
+    doubled = table * doubling.reshape(everyone, chunks, part * 4, 1)
+    table, doubled = lax.optimization_barrier((table, doubled))
+    forward_tables = [
+        table[:, g].reshape(everyone * part * 4, lon_count) for g in range(chunks)
+    ]
+    inverse_tables = [
+        doubled[:, g].reshape(everyone * part * 4, lon_count) for g in range(chunks)
+    ]
+
+    lev_index = lax.axis_index("lev")
+    first_slot = lax.axis_index("wave") * slot_count + lev_index * own
+    own_pairs = lax.dynamic_slice_in_dim(pair_of_slot, first_slot, own)
+    own_legendre = lax.dynamic_slice_in_dim(
+        legendre, lev_index * (own * col_count), own * col_count, axis=1
+    )
+    chooser = (
+        latitude_of_row[:, None] == jnp.arange(half_count, dtype=jnp.int32)[None, :]
+    ).astype(jnp.bfloat16)
+    own_rows = jnp.dot(chooser, own_legendre, preferred_element_type=jnp.float32).astype(
+        jnp.bfloat16
+    )
+    row_weight = jnp.take(gauss_weight, latitude_of_row, axis=0)
+    own_total, own_first = total_wave(own_pairs, lat_count)
+    own_factors = (own_total * (own_total + 1)).astype(jnp.float32) / float(
+        (lat_count - 1) * lat_count
+    )
+
+    def send(piece):
+        return lax.all_to_all(piece, ("wave", "lev"), split_axis=0, concat_axis=0, tiled=True)
+
+    def analyse(field_grid, g):
+        flat = field_grid.reshape(rows, lon_count)
+        coded = lax.dot_general(
+            forward_tables[g], flat, (((1,), (1,)), ((), ())), preferred_element_type=jnp.float32
+        ).astype(jnp.bfloat16)
+        return send(coded.reshape(everyone, part * 4, rows))
+
+    def chunk_rows(g):
+        taken = [
+            own_rows[:, (g * part + n) * col_count : (g * part + n + 1) * col_count]
+            for n in range(part)
+        ]
+        taken = jnp.stack(taken, axis=0)
+        return (taken[..., :even_cols], taken[..., even_cols:])
+
+    def forward(arrived, g):
+        even_rows, odd_rows = tables_of[g]
+        first = first_here[g * part : (g + 1) * part]
+        value = arrived.reshape(
+            wave_count, level_shards, part, 4, 2, lev_local, lat_pairs
+        ).transpose(4, 2, 3, 1, 5, 0, 6)
+        value = value.reshape(2, part, 4 * levels, half_count)
+        value = lax.optimization_barrier(value).astype(jnp.float32)
+        symmetric = (weight_here * (value[0] + value[1])).astype(jnp.bfloat16)
+        antisymmetric = (weight_here * (value[0] - value[1])).astype(jnp.bfloat16)
+        even_spec = jnp.einsum(
+            "jnq,jqc->jnc", symmetric, even_rows, preferred_element_type=jnp.float32
+        )
+        odd_spec = jnp.einsum(
+            "jnq,jqc->jnc", antisymmetric, odd_rows, preferred_element_type=jnp.float32
+        )
+        even_spec = even_spec.reshape(part, 2, 2, levels, even_cols)
+        odd_spec = odd_spec.reshape(part, 2, 2, levels, col_count - even_cols)
+        pick_even = first[:, None, None, :even_cols]
+        pick_odd = first[:, None, None, even_cols:]
+        even_pick = jnp.where(pick_even, even_spec[:, :, 0], even_spec[:, :, 1])
+        odd_pick = jnp.where(pick_odd, odd_spec[:, :, 0], odd_spec[:, :, 1])
+        return (
+            even_pick.astype(jnp.bfloat16).reshape(2 * part, levels, even_cols),
+            odd_pick.astype(jnp.bfloat16).reshape(2 * part, levels, col_count - even_cols),
+        )
+
+    def inverse(solved_even, solved_odd, g):
+        even_rows, odd_rows = tables_of[g]
+        first = first_here[g * part : (g + 1) * part]
+        mask = jnp.stack([first, jnp.logical_not(first)], axis=1)
+
+        def sums(solved, keep, table_rows):
+            value = solved.reshape(part, 2, 1, levels, solved.shape[-1])
+            masked = jnp.where(keep[:, None, :, None, :], value, jnp.zeros((), value.dtype))
+            masked = masked.reshape(part, 4 * levels, solved.shape[-1])
+            return jnp.einsum(
+                "jnc,jqc->jnq", masked, table_rows, preferred_element_type=jnp.float32
+            )
+
+        even_sum = sums(solved_even, mask[..., :even_cols], even_rows)
+        odd_sum = sums(solved_odd, mask[..., even_cols:], odd_rows)
+        both = jnp.stack([even_sum + odd_sum, even_sum - odd_sum], axis=0).astype(jnp.bfloat16)
+        both = both.reshape(2, part, 4, level_shards, lev_local, wave_count, lat_pairs)
+        both = both.transpose(5, 3, 1, 2, 0, 4, 6).reshape(everyone, part * 4, rows)
+        return both
+
+    tables_of = [chunk_rows(g) for g in range(chunks)]
+    arrived = [(analyse(div_grid, g), analyse(temp_grid, g)) for g in range(chunks)]
+    leaving = []
+    shared = (
+        g_matrix,
+        modes_in,
+        modes_out,
+        mode_rates,
+        temp_coupling,
+        row_weight,
+        own_first,
+        own_factors,
+    )
+    for g in range(chunks):
+        held, shared_here = lax.optimization_barrier((arrived[g], shared))
+        *matrices, weight_here, first_here, factors_here = shared_here
+        div_even, div_odd = forward(held[0], g)
+        temp_even, temp_odd = forward(held[1], g)
+        factors = jnp.repeat(factors_here[g * part : (g + 1) * part], 2, axis=0)
+        div_even, temp_even = vertical_solve(div_even, temp_even, factors[:, :even_cols], *matrices)
+        div_odd, temp_odd = vertical_solve(
+            div_odd, temp_odd, factors[:, even_cols:], *matrices
+        )
+        div_leaving = inverse(div_even, div_odd, g)
+        temp_leaving = inverse(temp_even, temp_odd, g)
+        leaving.append((div_leaving, temp_leaving))
+    returned = [(send(leaving[g][0]), send(leaving[g][1])) for g in range(chunks)]
+
+    def synthesise(field):
+        total = None
+        for g in range(chunks):
+            home = returned[g][field].reshape(everyone * part * 4, rows)
+            term = lax.dot_general(
+                home,
+                inverse_tables[g],
+                (((0,), (0,)), ((), ())),
+                preferred_element_type=jnp.float32,
+            )
+            total = term if total is None else total + term
+        return total.reshape(batches, 2, lev_local, lat_pairs, lon_count)
+
+    return (synthesise(0), synthesise(1))
+
+
 def solution(mesh):
     in_specs = (
         P(None, None, "lev", "wave", None),
@@ -203,6 +418,7 @@
         P(),
     )
     out_specs = (P(None, None, "lev", "wave", None), P(None, None, "lev", "wave", None))
+
     return jax.shard_map(
         per_device, mesh=mesh, in_specs=in_specs, out_specs=out_specs, check_vma=False
     )

time: 842 us -> 773 us (0.918)
  waiting for transfers between devices: 275 us -> 200 us
  matrix products: 140 us -> 92.1 us
  local copies, waits for them, and re-layouts: 324 us -> 350 us
  starting transfers between devices: 39.9 us -> 53.2 us
  other arithmetic: 50.1 us -> 63.2 us
    reshape x0 -> x22, local copies, waits for them, and re-layouts: none -> 195 us  [the longest x8 100 us: forward(): arrived.reshape(wave_count, level_shards, part, 4, 2, lev_local, lat_pairs)]
    all_to_all x12 -> x0, local copies, waits for them, and re-layouts: 83.4 us -> none  [the longest x3 18.8 us: per_device(): lax.all_to_all(div_fourier, 'wave', split_axis=3, concat_axis=4, tiled=True)]
    all_to_all x8, waiting for transfers between devices: 275 us -> 200 us  [send(): lax.all_to_all(piece, ('wave', 'lev'), split_axis=0, concat_axis=0, tiled...]
    unnamed x51 -> x103, local copies, waits for them, and re-layouts: 84.4 us -> 9.39 us
    convert_element_type x8 -> x2, local copies, waits for them, and re-layouts: 69.2 us -> 0.28 us  [transform_table(): doubling = jnp.where(wavenum == 0, 1.0, 2.0).astype(jnp.bfloat16)]
    another operation x5 -> x18, local copies, waits for them, and re-layouts: 18.5 us -> 87.2 us  [the longest x16 86.6 us: inverse(): jnp.stack([even_sum + odd_sum, even_sum - odd_sum], axis=0)]
    gather x4 -> x0, local copies, waits for them, and re-layouts: 42.2 us -> none  [the longest x3 41.6 us: per_device(): jnp.take(legendre, latitude_of_row, axis=0)]
    dot_general x8 -> x17, matrix products: 108 us -> 67.8 us  [the longest x4 28 us: synthesise(): lax.dot_general(home, inverse_tables[g], (((0,), (0,)), ((), ())), prefer...]
where the time goes in v1:
time: 773 us; the launch traced here: 760 us
  local copies, waits for them, and re-layouts  350 us (45%)
  waiting for transfers between devices  200 us (26%)
  matrix products  92.1 us (12%)
  other arithmetic  63.2 us (8%)
  starting transfers between devices  53.2 us (7%)
    all_to_all x8, waiting for transfers between devices, send(): lax.all_to_all(piece, ('wave', 'lev'), split_axis=0, concat_axis=0, tiled...  200 us
    reshape x8, local copies, waits for them, and re-layouts, forward(): arrived.reshape(wave_count, level_shards, part, 4, 2, lev_local, lat_pairs)  100 us
    another operation x16, local copies, waits for them, and re-layouts, inverse(): jnp.stack([even_sum + odd_sum, even_sum - odd_sum], axis=0)  86.6 us
    all_to_all x8, starting transfers between devices, send(): lax.all_to_all(piece, ('wave', 'lev'), split_axis=0, concat_axis=0, tiled...  53.2 us
    reshape x4, local copies, waits for them, and re-layouts, inverse(): both = both.transpose(5, 3, 1, 2, 0, 4, 6).reshape(everyone, part * 4, rows)  48.4 us
    reshape x4, local copies, waits for them, and re-layouts, forward(): value = value.reshape(2, part, 4 * levels, half_count)  40.1 us
    transpose x4, other arithmetic, inverse(): both = both.transpose(5, 3, 1, 2, 0, 4, 6).reshape(everyone, part * 4, rows)  28.8 us
    dot_general x4, matrix products, synthesise(): lax.dot_general(home, inverse_tables[g], (((0,), (0,)), ((), ())), prefer...  28 us
  transfers between devices with their start and end apart: 8, of which 7 were waited for; matrix products, arithmetic and copies ran while one was open for 30% of the time, Pallas kernels for 0%

profile of v1, /device:TPU:0, one launch (start us, length us, event | category | flops | bytes accessed | tf_op | source)
XLA Modules:
  0.0 760.2 jit_solution(1280001044518480477)
XLA Ops:
  17.6 7.3 all-to-all-start.1
  24.9 6.2 convolution_convert_fusion.4
  31.1 42.5 %all-to-all-done.1 = bf16[32,16,2048]{2,1,0:T(8,128)(2,1)S(1)} async-done(((bf16[32,16,2048]{2,1,0:T(8,128)(2,1)}), bf16[32,16,2048]{2,1,0:T(8,128)(2,1)S(1)}, u32[]{:S(2)}, u32[]{:S(2)}) %all-to-all-start.1) | async-done | bytes 2097184 | tf_op jit(solution)/shard_map/all_to_all | solution.py:298
  79.1 5.9 convolution_convert_fusion.1
  85.0 42.8 %all-to-all-done = bf16[32,16,2048]{2,1,0:T(8,128)(2,1)} async-done(((bf16[32,16,2048]{2,1,0:T(8,128)(2,1)}), bf16[32,16,2048]{2,1,0:T(8,128)(2,1)}, u32[]{:S(2)}, u32[]{:S(2)}) %all-to-all-start) | async-done | bytes 2097184 | tf_op jit(solution)/shard_map/all_to_all | solution.py:298
  127.8 15.8 %all-to-all-start.4 = ((bf16[32,16,2048]{2,1,0:T(8,128)(2,1)}), bf16[32,16,2048]{2,1,0:T(8,128)(2,1)S(1)}, u32[]{:S(2)}, u32[]{:S(2)}) async-start(bf16[32,16,2048]{2,1,0:T(8,128)(2,1)} %bitcast.383), calls=%async_computation.4 | async-start | bytes 4194304 | tf_op jit(solution)/shard_map/all_to_all | solution.py:298
  143.6 5.9 convolution_convert_fusion.2
  149.5 42.5 %all-to-all-done.4 = bf16[32,16,2048]{2,1,0:T(8,128)(2,1)S(1)} async-done(((bf16[32,16,2048]{2,1,0:T(8,128)(2,1)}), bf16[32,16,2048]{2,1,0:T(8,128)(2,1)S(1)}, u32[]{:S(2)}, u32[]{:S(2)}) %all-to-all-start.4) | async-done | bytes 2097184 | tf_op jit(solution)/shard_map/all_to_all | solution.py:298
  204.7 41.5 %all-to-all-done.3 = bf16[32,16,2048]{2,1,0:T(8,128)(2,1)S(1)} async-done(((bf16[32,16,2048]{2,1,0:T(8,128)(2,1)}), bf16[32,16,2048]{2,1,0:T(8,128)(2,1)S(1)}, u32[]{:S(2)}, u32[]{:S(2)}) %all-to-all-start.3) | async-done | bytes 2097184 | tf_op jit(solution)/shard_map/all_to_all | solution.py:298
  246.5 7.9 %reshape.397 = bf16[8,4,4,4,2,32,32]{6,5,4,3,2,1,0:T(8,128)(2,1)} reshape(bf16[32,16,2048]{2,1,0:T(8,128)(2,1)S(1)} %all-to-all-done.3) | data formatting | bytes 4194304 | tf_op jit(solution)/shard_map/reshape | solution.py:318
  254.4 16.5 %copy.116 = bf16[8,4,4,4,2,32,32]{6,0,5,1,3,2,4:T(8,128)(2,1)} copy(bf16[8,4,4,4,2,32,32]{6,5,4,3,2,1,0:T(8,128)(2,1)} %reshape.397) | data formatting | bytes 4194304 | tf_op jit(solution)/shard_map/reshape | solution.py:318
  270.9 10.1 %reshape.398 = bf16[2,4,512,256]{3,2,1,0:T(8,128)(2,1)S(1)} reshape(bf16[2,4,4,4,32,8,32]{6,5,4,3,2,1,0:T(8,128)(2,1)} %bitcast.360) | data formatting | bytes 4194304 | tf_op jit(solution)/shard_map/reshape | solution.py:321
  284.7 7.9 %reshape.401 = bf16[8,4,4,4,2,32,32]{6,5,4,3,2,1,0:T(8,128)(2,1)} reshape(bf16[32,16,2048]{2,1,0:T(8,128)(2,1)S(1)} %copy-done.15) | data formatting | bytes 4194304 | tf_op jit(solution)/shard_map/reshape | solution.py:318
  292.6 16.5 %copy.115 = bf16[8,4,4,4,2,32,32]{6,0,5,1,3,2,4:T(8,128)(2,1)} copy(bf16[8,4,4,4,2,32,32]{6,5,4,3,2,1,0:T(8,128)(2,1)} %reshape.401) | data formatting | bytes 4194304 | tf_op jit(solution)/shard_map/reshape | solution.py:318
  309.1 9.9 %reshape.402 = bf16[2,4,512,256]{3,2,1,0:T(8,128)(2,1)S(1)} reshape(bf16[2,4,4,4,32,8,32]{6,5,4,3,2,1,0:T(8,128)(2,1)} %bitcast.361) | data formatting | bytes 4194304 | tf_op jit(solution)/shard_map/reshape | solution.py:321
  322.4 10.5 %reshape.384 = bf16[8,4,4,4,2,32,32]{6,5,4,3,2,1,0:T(8,128)(2,1)} reshape(bf16[32,16,2048]{2,1,0:T(8,128)(2,1)} %all-to-all-done) | data formatting | bytes 4194304 | tf_op jit(solution)/shard_map/reshape | solution.py:318
  332.9 16.5 %copy.118 = bf16[8,4,4,4,2,32,32]{6,0,5,1,3,2,4:T(8,128)(2,1)} copy(bf16[8,4,4,4,2,32,32]{6,5,4,3,2,1,0:T(8,128)(2,1)} %reshape.384) | data formatting | bytes 4194304 | tf_op jit(solution)/shard_map/reshape | solution.py:318
  349.4 10.1 %reshape.385 = bf16[2,4,512,256]{3,2,1,0:T(8,128)(2,1)S(1)} reshape(bf16[2,4,4,4,32,8,32]{6,5,4,3,2,1,0:T(8,128)(2,1)} %bitcast.362) | data formatting | bytes 4194304 | tf_op jit(solution)/shard_map/reshape | solution.py:321
  363.3 7.9 %reshape.388 = bf16[8,4,4,4,2,32,32]{6,5,4,3,2,1,0:T(8,128)(2,1)} reshape(bf16[32,16,2048]{2,1,0:T(8,128)(2,1)S(1)} %copy-done.13) | data formatting | bytes 4194304 | tf_op jit(solution)/shard_map/reshape | solution.py:318
  371.2 16.5 %copy.117 = bf16[8,4,4,4,2,32,32]{6,0,5,1,3,2,4:T(8,128)(2,1)} copy(bf16[8,4,4,4,2,32,32]{6,5,4,3,2,1,0:T(8,128)(2,1)} %reshape.388) | data formatting | bytes 4194304 | tf_op jit(solution)/shard_map/reshape | solution.py:318
  387.7 9.9 %reshape.389 = bf16[2,4,512,256]{3,2,1,0:T(8,128)(2,1)S(1)} reshape(bf16[2,4,4,4,32,8,32]{6,5,4,3,2,1,0:T(8,128)(2,1)} %bitcast.363) | data formatting | bytes 4194304 | tf_op jit(solution)/shard_map/reshape | solution.py:321
  443.8 6.4 broadcast_select_fusion
  455.7 5.8 stack.127
  470.1 5.5 copy.102
  475.6 7.2 maximum_bitcast_fusion.3
  482.8 12.1 %reshape.411 = bf16[32,16,2048]{2,1,0:T(8,128)(2,1)} reshape(bf16[8,4,4,4,2,32,32]{6,5,4,3,2,1,0:T(8,128)(2,1)} %maximum_bitcast_fusion.3) | data formatting | bytes 4194304 | tf_op jit(solution)/shard_map/reshape | solution.py:359
  529.6 6.4 broadcast_select_fusion.2
  544.2 5.9 stack.110
  555.4 5.8 stack.111
  561.2 5.5 copy.73
  566.6 7.2 maximum_bitcast_fusion
  573.9 12.1 %reshape.393 = bf16[32,16,2048]{2,1,0:T(8,128)(2,1)} reshape(bf16[8,4,4,4,2,32,32]{6,5,4,3,2,1,0:T(8,128)(2,1)} %maximum_bitcast_fusion) | data formatting | bytes 4194304 | tf_op jit(solution)/shard_map/reshape | solution.py:359
  586.0 6.3 all-to-all-start.2
  598.6 5.8 stack.124
  609.6 5.8 stack.125
  620.8 7.2 maximum_bitcast_fusion.2
  628.0 12.1 %reshape.409 = bf16[32,16,2048]{2,1,0:T(8,128)(2,1)} reshape(bf16[8,4,4,4,2,32,32]{6,5,4,3,2,1,0:T(8,128)(2,1)} %maximum_bitcast_fusion.2) | data formatting | bytes 4194304 | tf_op jit(solution)/shard_map/reshape | solution.py:359
  640.9 5.6 all-to-all-start.6
  653.0 5.8 stack.121
  664.0 5.8 stack.122
  669.7 5.5 copy.92
  675.2 7.2 maximum_bitcast_fusion.1
  682.4 12.1 %reshape.406 = bf16[32,16,2048]{2,1,0:T(8,128)(2,1)} reshape(bf16[8,4,4,4,2,32,32]{6,5,4,3,2,1,0:T(8,128)(2,1)} %maximum_bitcast_fusion.1) | data formatting | bytes 4194304 | tf_op jit(solution)/shard_map/reshape | solution.py:359
  695.1 5.7 all-to-all-start.5
  707.0 7.4 fusion.118
  714.4 6.0 convolution_add_fusion
  720.4 29.1 %all-to-all-done.5 = bf16[32,16,2048]{2,1,0:T(8,128)(2,1)} async-done(((bf16[32,16,2048]{2,1,0:T(8,128)(2,1)}), bf16[32,16,2048]{2,1,0:T(8,128)(2,1)}, u32[]{:S(2)}, u32[]{:S(2)}) %all-to-all-start.5) | async-done | bytes 2097184 | tf_op jit(solution)/shard_map/all_to_all | solution.py:298
  749.5 10.1 %convolution_add_fusion.1 = f32[2048,1024]{1,0:T(8,128)} fusion(f32[2048,1024]{1,0:T(8,128)} %fusion.118, bf16[512,2048]{1,0:T(8,128)(2,1)} %bitcast.106, bf16[512,1024]{1,0:T(8,128)(2,1)} %bitcast.368), kind=kOutput, calls=%fused_computation.11 | convolution fusion | flops 2149580800 | bytes 19922944 | tf_op jit(solution)/shard_map/dot_general | solution.py:394
  (262 shorter events, 190.4 us)
Async XLA Ops:
  0.6 428.2 %copy-start = (f32[128,128]{1,0:T(8,128)S(1)}, f32[128,128]{1,0:T(8,128)}, u32[]{:S(2)}) copy-start(f32[128,128]{1,0:T(8,128)} %param.19) | copy-start | bytes 196612
  11.3 2.6 copy-start.43
  11.5 6.1 copy-start.39
  17.6 56.0 %all-to-all-start.1 = ((bf16[32,16,2048]{2,1,0:T(8,128)(2,1)}), bf16[32,16,2048]{2,1,0:T(8,128)(2,1)S(1)}, u32[]{:S(2)}, u32[]{:S(2)}) async-start(bf16[32,16,2048]{2,1,0:T(8,128)(2,1)} %bitcast.384), calls=%async_computation.1 | async-start | bytes 4194304 | tf_op jit(solution)/shard_map/all_to_all | solution.py:298
  75.0 52.8 %all-to-all-start = ((bf16[32,16,2048]{2,1,0:T(8,128)(2,1)}), bf16[32,16,2048]{2,1,0:T(8,128)(2,1)}, u32[]{:S(2)}, u32[]{:S(2)}) async-start(bf16[32,16,2048]{2,1,0:T(8,128)(2,1)} %bitcast.382), calls=%async_computation | async-start | bytes 4194304 | tf_op jit(solution)/shard_map/all_to_all | solution.py:298
  127.8 64.2 %all-to-all-start.4 = ((bf16[32,16,2048]{2,1,0:T(8,128)(2,1)}), bf16[32,16,2048]{2,1,0:T(8,128)(2,1)S(1)}, u32[]{:S(2)}, u32[]{:S(2)}) async-start(bf16[32,16,2048]{2,1,0:T(8,128)(2,1)} %bitcast.383), calls=%async_computation.4 | async-start | bytes 4194304 | tf_op jit(solution)/shard_map/all_to_all | solution.py:298
  193.4 4.1 copy-start.40
  193.4 4.1 copy-start.1
  193.4 6.1 copy-start.41
  193.4 52.8 %all-to-all-start.3 = ((bf16[32,16,2048]{2,1,0:T(8,128)(2,1)}), bf16[32,16,2048]{2,1,0:T(8,128)(2,1)S(1)}, u32[]{:S(2)}, u32[]{:S(2)}) async-start(bf16[32,16,2048]{2,1,0:T(8,128)(2,1)} %bitcast.381), calls=%async_computation.3 | async-start | bytes 4194304 | tf_op jit(solution)/shard_map/all_to_all | solution.py:298
  202.7 195.3 %copy-start.8 = (bf16[4,256,256]{1,2,0:T(8,128)(2,1)}, bf16[4,256,256]{1,2,0:T(8,128)(2,1)S(1)}, u32[]{:S(2)}) copy-start(bf16[4,256,256]{1,2,0:T(8,128)(2,1)S(1)} %get-tuple-element.172) | copy-start | bytes 1572868
  202.7 232.4 %copy-start.6 = (bf16[4,256,256]{1,2,0:T(8,128)(2,1)}, bf16[4,256,256]{1,2,0:T(8,128)(2,1)S(1)}, u32[]{:S(2)}) copy-start(bf16[4,256,256]{1,2,0:T(8,128)(2,1)S(1)} %get-tuple-element.171) | copy-start | bytes 1572868
  282.9 1.9 copy-start.15
  319.4 1.5 copy-start.18
  359.9 1.5 copy-start.21
  361.4 1.9 copy-start.13
  398.0 1.5 copy-start.22
  401.0 2.1 copy-start.30
  408.7 2.4 copy-start.31
  418.7 1.6 copy-start.29
  421.3 4.2 copy-start.36
  421.3 4.2 copy-start.37
  423.5 3.7 copy-start.38
  425.5 2.2 copy-start.44
  425.5 2.2 copy-start.47
  443.8 8.6 %copy-start.16 = (f32[4,512,256]{2,1,0:T(8,128)S(1)}, f32[4,512,256]{2,1,0:T(8,128)}, u32[]{:S(2)}) copy-start(f32[4,512,256]{2,1,0:T(8,128)} %fusion.122) | copy-start | bytes 6291460
  443.8 8.6 %copy-start.19 = (bf16[4,256,513]{1,2,0:T(8,128)(2,1)S(1)}, bf16[4,256,513]{1,2,0:T(8,128)(2,1)}, u32[]{:S(2)}) copy-start(bf16[4,256,513]{1,2,0:T(8,128)(2,1)} %get-tuple-element.170) | copy-start | bytes 3151876
  461.5 5.4 copy-start.28
  470.1 5.5 copy-start.2
  494.9 91.1 %all-to-all-start.7 = ((bf16[32,16,2048]{2,1,0:T(8,128)(2,1)}), bf16[32,16,2048]{2,1,0:T(8,128)(2,1)S(1)}, u32[]{:S(2)}, u32[]{:S(2)}) async-start(bf16[32,16,2048]{2,1,0:T(8,128)(2,1)} %reshape.411), calls=%async_computation.7 | async-start | bytes 4194304 | tf_op jit(solution)/shard_map/all_to_all | solution.py:298
  499.3 6.4 copy-start.34
  505.7 2.2 copy-start.46
  529.6 8.6 %copy-start.35 = (bf16[4,2,128,256]{3,2,1,0:T(8,128)(2,1)S(1)}, bf16[4,2,128,256]{3,2,1,0:T(8,128)(2,1)}, u32[]{:S(2)}) copy-start(bf16[4,2,128,256]{3,2,1,0:T(8,128)(2,1)} %copy.94) | copy-start | bytes 1572868
  538.2 2.2 copy-start.9
  540.5 1.6 copy-start.25
  561.2 5.5 copy-start.3
  586.0 55.0 %all-to-all-start.2 = ((bf16[32,16,2048]{2,1,0:T(8,128)(2,1)}), bf16[32,16,2048]{2,1,0:T(8,128)(2,1)}, u32[]{:S(2)}, u32[]{:S(2)}) async-start(bf16[32,16,2048]{2,1,0:T(8,128)(2,1)} %reshape.393), calls=%async_computation.2 | async-start | bytes 4194304 | tf_op jit(solution)/shard_map/all_to_all | solution.py:298
  592.2 2.3 copy-start.10
  594.6 1.8 copy-start.24
  594.6 1.9 copy-start.26
  615.4 5.5 copy-start.4
  640.9 54.2 %all-to-all-start.6 = ((bf16[32,16,2048]{2,1,0:T(8,128)(2,1)}), bf16[32,16,2048]{2,1,0:T(8,128)(2,1)}, u32[]{:S(2)}, u32[]{:S(2)}) async-start(bf16[32,16,2048]{2,1,0:T(8,128)(2,1)} %reshape.409), calls=%async_computation.6 | async-start | bytes 4194304 | tf_op jit(solution)/shard_map/all_to_all | solution.py:298
  646.5 2.3 copy-start.7
  648.8 1.8 copy-start.20
  648.8 1.9 copy-start.27
  669.7 5.5 copy-start.5
  695.1 54.4 %all-to-all-start.5 = ((bf16[32,16,2048]{2,1,0:T(8,128)(2,1)}), bf16[32,16,2048]{2,1,0:T(8,128)(2,1)}, u32[]{:S(2)}, u32[]{:S(2)}) async-start(bf16[32,16,2048]{2,1,0:T(8,128)(2,1)} %reshape.406), calls=%async_computation.5 | async-start | bytes 4194304 | tf_op jit(solution)/shard_map/all_to_all | solution.py:298
  702.6 11.8 %copy-start.11 = (bf16[32,1,16,1024]{3,2,1,0:T(8,128)(2,1)}, bf16[32,1,16,1024]{3,2,1,0:T(8,128)(2,1)S(1)}, u32[]{:S(2)}) copy-start(bf16[32,1,16,1024]{3,2,1,0:T(8,128)(2,1)S(1)} %get-tuple-element.72) | copy-start | bytes 3145732
  (8 other events, 10.0 us)
